TPU v7x, 32 devices: a whole 2x2x4 slice. The times are simulated.
32 devices in a mesh: dp: 4 (over y, core), row: 2 (over x), col: 4 (over z).
Axes of the slice: x: 2, y: 2, z: 4, core: 2. Of those that a mesh axis runs over, the one named last changes fastest.
Arguments:
- inputs: bfloat16 [2048, 6144], P('dp', 'row'), may hold values from -600 to 600
- saved_qkv: bfloat16 [2048, 3, 3072], P('dp', None, 'col'), may hold values from -6 to 6
- saved_up: bfloat16 [2048, 12288], P('dp', 'col'), may hold values from -6 to 6
- cotangent: bfloat16 [2048, 6144], P('dp', 'row'), may hold values from -6 to 6
- weight_qkv: bfloat16 [6144, 3, 3072], P('row', None, 'col'), may hold values from -0.078125 to 0.078125
- weight_up: bfloat16 [6144, 12288], P('row', 'col'), may hold values from -0.078125 to 0.078125
- weight_attn: bfloat16 [3072, 6144], P('col', 'row'), may hold values from -0.109375 to 0.109375
- weight_down: bfloat16 [12288, 6144], P('col', 'row'), may hold values from -0.0546875 to 0.0546875
Outputs:
- grad_inputs: bfloat16 [2048, 6144], P(('dp', 'col'), 'row')
- grad_qkv: bfloat16 [2, 4, 768, 3, 3072], P('row', 'dp', None, None, 'col')
- grad_up: bfloat16 [2, 4, 768, 12288], P('row', 'dp', None, 'col')
- grad_attn: bfloat16 [4, 4, 192, 6144], P('col', 'dp', None, 'row')
- grad_down: bfloat16 [4, 4, 768, 6144], P('col', 'dp', None, 'row')
All inputs are finite; a program needn't handle non-finite values.
Results may differ from a plain program's by a relative error of at most 0.0039.
The roundings to bfloat16 on the way count: a program that leaves them out, or rounds other values in their place, can miss the bound.
Values may be sent and summed in bfloat16 or wider, within the bound.
No kernel may reach another device: no remote copies, remote signals or barrier semaphores. Data moves between devices by JAX's collectives and lax.ppermute only.
A program may use at most 192 MiB of HBM per device.

v0:
```python
import jax
import jax.numpy as jnp
from jax import lax
from jax.sharding import PartitionSpec as P

HD = 128
S = 256
EPS = 1e-06
SQRT_HALF = 0.7071067811865476
INV_ROOT_TWO_PI = 0.3989422804014327


def gelu_exact(values):
    return 0.5 * values * (1.0 + jax.scipy.special.erf(values * SQRT_HALF))


def gelu_slope(values):
    cumul = 0.5 * (1.0 + jax.scipy.special.erf(values * SQRT_HALF))
    return cumul + values * jnp.exp(-0.5 * values * values) * INV_ROOT_TWO_PI


def head_norm(values):
    average = jnp.mean(values, axis=-1, keepdims=True)
    centred = values - average
    inv_std = lax.rsqrt(jnp.mean(centred * centred, axis=-1, keepdims=True) + EPS)
    return (centred * inv_std, inv_std)


def head_norm_back(normed, inv_std, upstream):
    first = jnp.mean(upstream, axis=-1, keepdims=True)
    cross = jnp.mean(upstream * normed, axis=-1, keepdims=True)
    return inv_std * (upstream - first - normed * cross)


def body(inputs, saved_qkv, saved_up, cotangent, weight_qkv, weight_up, weight_attn, weight_down):
    f32 = jnp.float32
    bf16 = jnp.bfloat16
    tok_rows, feat_local = inputs.shape
    head_cols = saved_qkv.shape[2]
    up_cols = saved_up.shape[1]
    n_row = lax.axis_size("row")
    n_col = lax.axis_size("col")
    width = feat_local * n_row
    head_count = head_cols // HD
    images = tok_rows // S
    values = inputs.astype(f32)
    first_sum, square_sum = lax.psum(
        (jnp.sum(values, axis=1), jnp.sum(values * values, axis=1)), "row"
    )
    average = (first_sum / width)[:, None]
    inv_std = lax.rsqrt((square_sum / width)[:, None] - average * average + EPS)
    normed = (values - average) * inv_std
    normed_b = normed.astype(bf16)
    qkv5 = saved_qkv.reshape(images, S, 3, head_count, HD)
    query = qkv5[:, :, 0]
    keyed = qkv5[:, :, 1]
    valued = qkv5[:, :, 2]
    q_norm, q_inv = head_norm(query.astype(f32))
    k_norm, k_inv = head_norm(keyed.astype(f32))
    qn_b = q_norm.astype(bf16)
    kn_b = k_norm.astype(bf16)
    scale = HD ** (-0.5)
    scores = jnp.einsum("bqhd,bkhd->bhqk", qn_b, kn_b, preferred_element_type=f32) * scale
    expo = jnp.exp(scores)
    probs = expo / jnp.sum(expo, axis=-1, keepdims=True)
    probs_b = probs.astype(bf16)
    attended = jnp.einsum("bhqk,bkhd->bqhd", probs_b, valued, preferred_element_type=f32).astype(
        bf16
    )
    attended = attended.reshape(tok_rows, head_cols)
    hidden_b = gelu_exact(saved_up.astype(f32)).astype(bf16)
    part_attn = jnp.einsum("td,ad->ta", cotangent, weight_attn, preferred_element_type=f32)
    part_hidden = jnp.einsum("td,fd->tf", cotangent, weight_down, preferred_element_type=f32)
    sum_attn, sum_hidden = lax.psum((part_attn, part_hidden), "row")
    grad_o = sum_attn.astype(bf16)
    grad_pre = (sum_hidden * gelu_slope(saved_up.astype(f32))).astype(bf16)
    grad_o4 = grad_o.reshape(images, S, head_count, HD)
    grad_probs = jnp.einsum("bqhd,bkhd->bhqk", grad_o4, valued, preferred_element_type=f32)
    grad_value = jnp.einsum("bhqk,bqhd->bkhd", probs_b, grad_o4, preferred_element_type=f32).astype(
        bf16
    )
    rowdot = jnp.sum(probs * grad_probs, axis=-1, keepdims=True)
    grad_scores = (probs * (grad_probs - rowdot) * scale).astype(bf16)
    grad_qn = jnp.einsum("bhqk,bkhd->bqhd", grad_scores, kn_b, preferred_element_type=f32)
    grad_kn = jnp.einsum("bhqk,bqhd->bkhd", grad_scores, qn_b, preferred_element_type=f32)
    grad_query = head_norm_back(q_norm, q_inv, grad_qn).astype(bf16)
    grad_key = head_norm_back(k_norm, k_inv, grad_kn).astype(bf16)
    grad_flat = jnp.stack([grad_query, grad_key, grad_value], axis=2).reshape(
        tok_rows, 3 * head_cols
    )
    flat_weight = weight_qkv.reshape(feat_local, 3 * head_cols)
    share_rows = tok_rows // n_col
    total = jnp.einsum("ta,da->td", grad_flat, flat_weight, preferred_element_type=f32)
    grad_normed = lax.psum_scatter(
        total + jnp.einsum("tf,df->td", grad_pre, weight_up, preferred_element_type=f32),
        "col",
        scatter_dimension=0,
        tiled=True,
    )
    first_row = lax.axis_index("col") * share_rows
    normed_share = lax.dynamic_slice_in_dim(normed, first_row, share_rows, 0)
    inv_share = lax.dynamic_slice_in_dim(inv_std, first_row, share_rows, 0)
    cot_share = lax.dynamic_slice_in_dim(cotangent, first_row, share_rows, 0)
    sum_grad, sum_cross = lax.psum(
        (jnp.sum(grad_normed, axis=1), jnp.sum(grad_normed * normed_share, axis=1)), "row"
    )
    branch_term = (
        grad_normed - (sum_grad / width)[:, None] - normed_share * (sum_cross / width)[:, None]
    )
    grad_inputs = (cot_share.astype(f32) + inv_share * branch_term).astype(bf16)
    moved_normed, moved_attended, moved_hidden = (
        lax.all_to_all(normed_b, "dp", split_axis=1, concat_axis=0, tiled=True),
        lax.all_to_all(attended, "dp", split_axis=1, concat_axis=0, tiled=True),
        lax.all_to_all(hidden_b, "dp", split_axis=1, concat_axis=0, tiled=True),
    )
    cot_piece = lax.all_gather(cotangent, "dp", axis=0, tiled=True)
    flat_piece = lax.all_gather(grad_flat, "dp", axis=0, tiled=True)
    pre_piece = lax.all_gather(grad_pre, "dp", axis=0, tiled=True)
    new_qkv = jnp.einsum("td,ta->da", moved_normed, flat_piece, preferred_element_type=f32)
    new_up = jnp.einsum("td,tf->df", moved_normed, pre_piece, preferred_element_type=f32)
    new_attn = jnp.einsum("ta,td->ad", moved_attended, cot_piece, preferred_element_type=f32)
    new_down = jnp.einsum("tf,td->fd", moved_hidden, cot_piece, preferred_element_type=f32)
    grad_qkv = new_qkv.astype(bf16).reshape(1, 1, new_qkv.shape[0], 3, head_cols)
    grad_up = new_up.astype(bf16).reshape(1, 1, new_up.shape[0], up_cols)
    grad_attn = new_attn.astype(bf16).reshape(1, 1, new_attn.shape[0], feat_local)
    grad_down = new_down.astype(bf16).reshape(1, 1, new_down.shape[0], feat_local)
    return (grad_inputs, grad_qkv, grad_up, grad_attn, grad_down)


def solution(mesh):
    return jax.shard_map(
        body,
        mesh=mesh,
        in_specs=(
            P("dp", "row"),
            P("dp", None, "col"),
            P("dp", "col"),
            P("dp", "row"),
            P("row", None, "col"),
            P("row", "col"),
            P("col", "row"),
            P("col", "row"),
        ),
        out_specs=(
            P(("dp", "col"), "row"),
            P("row", "dp", None, None, "col"),
            P("row", "dp", None, "col"),
            P("col", "dp", None, "row"),
            P("col", "dp", None, "row"),
        ),
        check_vma=False,
    )
```

profile of v0, /device:TPU:0, one launch (start us, length us, event | category | flops | bytes accessed | tf_op | source)
XLA Modules:
  0.0 490.4 jit_solution(17388915969645549124)
XLA Ops:
  8.0 16.4 %fusion.87 = f32[512,3072]{1,0:T(8,128)} fusion(bf16[512,3072]{1,0:T(8,128)(2,1)} %param.11, bf16[3072,3072]{1,0:T(8,128)(2,1)} %param.15), kind=kOutput, calls=%fused_computation.110 | convolution fusion | flops 9663676416 | bytes 28311552 | tf_op jit(solution)/shard_map/td,fd->tf/dot_general | solution.py:73
  24.5 7.2 %fusion.85 = f32[512,768]{1,0:T(8,128)} fusion(bf16[512,3072]{1,0:T(8,128)(2,1)} %param.11, bf16[768,3072]{1,0:T(8,128)(2,1)} %param.14), kind=kOutput, calls=%fused_computation.108 | convolution fusion | flops 2415919104 | bytes 9437184 | tf_op jit(solution)/shard_map/td,ad->ta/dot_general | solution.py:72
  32.7 79.4 %all-reduce.6 = (bf16[512,768]{1,0:T(8,128)(2,1)S(1)}, f32[512]{0:T(512)S(1)}, f32[512]{0:T(512)S(1)}) all-reduce(f32[512,768]{1,0:T(8,128)} %fusion.85, f32[512]{0:T(512)S(1)} %get-tuple-element.16, f32[512]{0:T(512)S(1)} %get-tuple-element.15), channel_id=1, replica_groups=mesh['dp'=4,'row'=2,'col'=4] {'row'}, use_global_device_ids=true, to_apply=%region_9.0 | all-reduce | flops 394240 | bytes 2367488 | tf_op jit(solution)/shard_map/psum | solution.py:74
  113.7 2.8 copy.25
  118.7 3.8 fusion.80
  130.4 7.8 %bitcast_reduce_fusion = (f32[2,256,6]{1,2,0:T(8,128)S(1)}, f32[2,256,6]{1,2,0:T(8,128)S(1)}, f32[2,6,128,256]{3,2,1,0:T(8,128)}) fusion(f32[2,256,6]{1,2,0:T(8,128)S(1)} %add_rsqrt_fusion, f32[2,256,6]{1,2,0:T(8,128)S(1)} %broadcast_multiply_fusion.4, bf16[2,256,1,6,128]{1,0,4,3,2:T(2,128)(2,1)S(1)} %get-tuple-element.34, f32[2,6,256,256]{2,3,1,0:T(8,128)} %fusion.55, ...), kind=kOutput, calls=%fused_computation.66 | convolution fusion | flops 212333824 | bytes 9523200 | tf_op jit(solution)/shard_map/bhqk,bqhd->bkhd/dot_general | solution.py:85
  138.2 7.7 %bitcast_reduce_fusion.1 = (f32[2,256,6]{1,2,0:T(8,128)S(1)}, f32[2,256,6]{1,2,0:T(8,128)S(1)}, f32[2,6,128,256]{3,2,1,0:T(8,128)}) fusion(f32[2,256,6]{1,2,0:T(8,128)S(1)} %add_rsqrt_fusion.1, f32[2,256,6]{1,2,0:T(8,128)S(1)} %broadcast_multiply_fusion.5, bf16[2,256,1,6,128]{1,0,4,3,2:T(2,128)(2,1)S(1)} %get-tuple-element.33, ...), kind=kOutput, calls=%fused_computation.68 | convolution fusion | flops 212333824 | bytes 9523200 | tf_op jit(solution)/shard_map/bhqk,bkhd->bqhd/dot_general | solution.py:84
  154.7 19.4 %copy.38 = bf16[3072,3,768]{0,2,1:T(8,128)(2,1)} copy(bf16[3072,3,768]{2,0,1:T(8,128)(2,1)} %param.12) | data formatting | bytes 28311552 | tf_op args[4]
  174.1 12.6 %fusion.86 = f32[512,3072]{1,0:T(8,128)} fusion(bf16[512,2304]{0,1:T(8,128)(2,1)S(1)} %bitcast.152, bf16[3072,2304]{0,1:T(8,128)(2,1)} %bitcast.147), kind=kOutput, calls=%fused_computation.109 | convolution fusion | flops 7247757312 | bytes 22806528 | tf_op jit(solution)/shard_map/ta,da->td/dot_general | solution.py:93
  186.7 27.9 %all-reduce.5.cloned.1.call-done = f32[512,3072]{1,0:T(8,128)} async-done(((f32[512,3072]{1,0:T(8,128)}), f32[512,3072]{1,0:T(8,128)}) %all-reduce.5.cloned.1.call-update) | async-done | bytes 6291472 | tf_op jit(solution)/shard_map/psum | solution.py:74
  214.6 7.8 %fusion.11 = (bf16[512,3072]{1,0:T(8,128)(2,1)}, bf16[512,3072]{1,0:T(8,128)(2,1)S(1)}) fusion(bf16[512,3072]{1,0:T(8,128)(2,1)} %param.10, f32[512,3072]{1,0:T(8,128)} %all-reduce.5.cloned.1.call-done), kind=kLoop, calls=%fused_computation.19 | loop fusion | flops 22020096 | bytes 15728640 | tf_op jit(solution)/shard_map/convert_element_type | solution.py:71
  222.4 17.5 %convolution_add_fusion = f32[512,3072]{1,0:T(8,128)} fusion(f32[512,3072]{1,0:T(8,128)} %fusion.86, bf16[512,3072]{1,0:T(8,128)(2,1)S(1)} %get-tuple-element.31, bf16[3072,3072]{1,0:T(8,128)(2,1)} %param.13), kind=kOutput, calls=%fused_computation.23 | convolution fusion | flops 9665249280 | bytes 34603008 | tf_op jit(solution)/shard_map/tf,df->td/dot_general | solution.py:95
  241.2 3.6 fusion.51
  244.8 4.0 copy.42
  248.8 3.2 all_to_all.46
  252.0 4.7 all-to-all-start.1
  256.7 4.0 fusion.72
  262.6 14.6 %all-to-all-done.1 = bf16[512,4,192]{0,2,1:T(8,128)(2,1)} async-done(((bf16[512,4,192]{0,2,1:T(8,128)(2,1)}), bf16[512,4,192]{0,2,1:T(8,128)(2,1)}, u32[]{:S(2)}, u32[]{:S(2)}) %all-to-all-start.1) | async-done | bytes 786464 | tf_op jit(solution)/shard_map/all_to_all | solution.py:113
  277.2 4.9 %all-to-all-start = ((bf16[512,4,768]{2,0,1:T(8,128)(2,1)}), bf16[512,4,768]{2,0,1:T(8,128)(2,1)}, u32[]{:S(2)}, u32[]{:S(2)}) async-start(bf16[512,4,768]{2,0,1:T(8,128)(2,1)} %bitcast.146), calls=%async_computation.1 | async-start | bytes 6291456 | tf_op jit(solution)/shard_map/all_to_all | solution.py:112
  286.2 67.0 %all-to-all-done = bf16[512,4,768]{2,0,1:T(8,128)(2,1)} async-done(((bf16[512,4,768]{2,0,1:T(8,128)(2,1)}), bf16[512,4,768]{2,0,1:T(8,128)(2,1)}, u32[]{:S(2)}, u32[]{:S(2)}) %all-to-all-start) | async-done | bytes 3145760 | tf_op jit(solution)/shard_map/all_to_all | solution.py:112
  353.2 4.7 all-to-all-start.2
  357.9 13.2 %convolution_convert_fusion.2 = bf16[768,2304]{1,0:T(8,128)(2,1)} fusion(bf16[2048,768]{1,0:T(8,128)(2,1)} %bitcast.11, bf16[2048,2304]{0,1:T(8,128)(2,1)} %all-gather.4.cloned.1.call-done), kind=kOutput, calls=%fused_computation.22 | convolution fusion | flops 7249526784 | bytes 16121856 | tf_op jit(solution)/shard_map/td,ta->da/dot_general | solution.py:119
  371.1 4.5 copy.40
  375.6 3.7 copy.45
  379.3 2.7 fusion.79
  382.1 5.1 %all-reduce = (f32[128]{0:T(128)S(1)}, f32[128]{0:T(128)S(1)}) all-reduce(f32[128]{0:T(128)S(1)} %get-tuple-element.18, f32[128]{0:T(128)S(1)} %get-tuple-element.17), channel_id=1, replica_groups=mesh['dp'=4,'row'=2,'col'=4] {'row'}, use_global_device_ids=true, to_apply=%region_20.0 | all-reduce | flops 256 | bytes 2048 | tf_op jit(solution)/shard_map/psum | solution.py:104
  387.2 3.2 add_convert_fusion
  390.4 8.2 %fusion.14 = bf16[1,1,192,3072]{3,2,1,0:T(8,128)(2,1)} fusion(bf16[2048,192]{0,1:T(8,128)(2,1)S(1)} %bitcast.154, bf16[2048,3072]{1,0:T(8,128)(2,1)} %all-gather.8.cloned.1.call-done), kind=kOutput, calls=%fused_computation.27 | convolution fusion | flops 2416508928 | bytes 14548992 | tf_op jit(solution)/shard_map/ta,td->ad/dot_general | solution.py:121
  398.6 11.4 %all-to-all-done.2 = bf16[512,4,768]{2,0,1:T(8,128)(2,1)} async-done(((bf16[512,4,768]{2,0,1:T(8,128)(2,1)}), bf16[512,4,768]{2,0,1:T(8,128)(2,1)}, u32[]{:S(2)}, u32[]{:S(2)}) %all-to-all-start.2) | async-done | bytes 3145760 | tf_op jit(solution)/shard_map/all_to_all | solution.py:114
  410.0 15.5 %fusion.13 = bf16[1,1,768,3072]{3,2,1,0:T(8,128)(2,1)} fusion(bf16[2048,768]{1,0:T(8,128)(2,1)} %bitcast.19, bf16[2048,3072]{1,0:T(8,128)(2,1)} %all-gather.8.cloned.1.call-done), kind=kOutput, calls=%fused_computation.25 | convolution fusion | flops 9666035712 | bytes 20447232 | tf_op jit(solution)/shard_map/tf,td->fd/dot_general | solution.py:122
  425.5 41.8 %all-gather.6.cloned.1.call-done = bf16[2048,3072]{1,0:T(8,128)(2,1)} async-done(((bf16[512,3072]{1,0:T(8,128)(2,1)}), bf16[2048,3072]{1,0:T(8,128)(2,1)}) %all-gather.6.cloned.1.call-update) | async-done | bytes 12582928 | tf_op jit(solution)/shard_map/all_gather | solution.py:118
  467.3 15.3 %fusion.12 = bf16[1,1,768,3072]{3,2,1,0:T(8,128)(2,1)} fusion(bf16[2048,768]{1,0:T(8,128)(2,1)} %bitcast.11, bf16[2048,3072]{1,0:T(8,128)(2,1)} %all-gather.6.cloned.1.call-done), kind=kOutput, calls=%fused_computation.24 | convolution fusion | flops 9666035712 | bytes 20447232 | tf_op jit(solution)/shard_map/td,tf->df/dot_general | solution.py:120
  (66 shorter events, 28.4 us)
Async XLA Ops:
  8.0 206.6 %all-reduce.5.cloned.1.call-start = ((), (), s32[]{:S(2)}) async-start(), calls=%async_computation.4 | async-start | bytes 12582912 | tf_op jit(solution)/shard_map/psum | solution.py:74
  24.4 7.3 %copy-start = (bf16[512,3072]{1,0:T(8,128)(2,1)S(1)}, bf16[512,3072]{1,0:T(8,128)(2,1)}, u32[]{:S(2)}) copy-start(bf16[512,3072]{1,0:T(8,128)(2,1)} %param.8) | copy-start | bytes 9437188
  24.5 333.5 %all-gather.4.cloned.1.call-start = ((), (), s32[]{:S(2)}) async-start(), calls=%async_computation.6 | async-start | bytes 11796480 | tf_op jit(solution)/shard_map/all_gather | solution.py:117
  124.9 2.9 copy-start.6
  145.9 2.2 copy-start.8
  145.9 3.3 copy-start.10
  154.6 19.5 %copy-start.4 = (bf16[288,8,2,256]{3,1,2,0:T(8,128)(2,1)S(1)}, bf16[288,8,2,256]{3,1,2,0:T(8,128)(2,1)}, u32[]{:S(2)}) copy-start(bf16[288,8,2,256]{3,1,2,0:T(8,128)(2,1)} %copy.60) | copy-start | bytes 7077892
  154.6 224.7 %reduce-scatter.2.cloned.1.call-start = ((), (), s32[]{:S(2)}) async-start(), calls=%async_computation.5 | async-start | bytes 7864320 | tf_op jit(solution)/shard_map/reduce_scatter | solution.py:94
  222.4 17.5 %copy-start.2 = (bf16[512,3072]{1,0:T(8,128)(2,1)}, bf16[512,3072]{1,0:T(8,128)(2,1)S(1)}, u32[]{:S(2)}) copy-start(bf16[512,3072]{1,0:T(8,128)(2,1)S(1)} %get-tuple-element.31) | copy-start | bytes 9437188
  240.0 1.2 copy-start.7
  240.0 150.4 %all-gather.8.cloned.1.call-start = ((), (), s32[]{:S(2)}) async-start(), calls=%async_computation.8 | async-start | bytes 15728640 | tf_op jit(solution)/shard_map/all_gather | solution.py:116
  240.6 226.7 %all-gather.6.cloned.1.call-start = ((), (), s32[]{:S(2)}) async-start(), calls=%async_computation.7 | async-start | bytes 15728640 | tf_op jit(solution)/shard_map/all_gather | solution.py:118
  244.8 11.9 %copy-start.1 = (bf16[512,3072]{1,0:T(8,128)(2,1)S(1)}, bf16[512,3072]{1,0:T(8,128)(2,1)}, u32[]{:S(2)}) copy-start(bf16[512,3072]{1,0:T(8,128)(2,1)} %param.8) | copy-start | bytes 9437188
  252.0 25.2 %all-to-all-start.1 = ((bf16[512,4,192]{0,2,1:T(8,128)(2,1)}), bf16[512,4,192]{0,2,1:T(8,128)(2,1)}, u32[]{:S(2)}, u32[]{:S(2)}) async-start(bf16[512,4,192]{0,2,1:T(8,128)(2,1)} %all_to_all.46), calls=%async_computation.2 | async-start | bytes 1572864 | tf_op jit(solution)/shard_map/all_to_all | solution.py:113
  277.2 7.1 %copy-start.3 = (bf16[512,3072]{1,0:T(8,128)(2,1)S(1)}, bf16[512,3072]{1,0:T(8,128)(2,1)}, u32[]{:S(2)}) copy-start(bf16[512,3072]{1,0:T(8,128)(2,1)} %get-tuple-element.30) | copy-start | bytes 9437188
  277.2 76.0 %all-to-all-start = ((bf16[512,4,768]{2,0,1:T(8,128)(2,1)}), bf16[512,4,768]{2,0,1:T(8,128)(2,1)}, u32[]{:S(2)}, u32[]{:S(2)}) async-start(bf16[512,4,768]{2,0,1:T(8,128)(2,1)} %bitcast.146), calls=%async_computation.1 | async-start | bytes 6291456 | tf_op jit(solution)/shard_map/all_to_all | solution.py:112
  353.2 56.7 %all-to-all-start.2 = ((bf16[512,4,768]{2,0,1:T(8,128)(2,1)}), bf16[512,4,768]{2,0,1:T(8,128)(2,1)}, u32[]{:S(2)}, u32[]{:S(2)}) async-start(bf16[512,4,768]{2,0,1:T(8,128)(2,1)} %bitcast.145), calls=%async_computation.3 | async-start | bytes 6291456 | tf_op jit(solution)/shard_map/all_to_all | solution.py:114
  379.3 7.8 %copy-start.5 = (f32[128,3072]{1,0:T(8,128)S(1)}, f32[128,3072]{1,0:T(8,128)}, u32[]{:S(2)}) copy-start(f32[128,3072]{1,0:T(8,128)} %reduce-scatter.2.cloned.1.call-done) | copy-start | bytes 4718596
  382.1 8.3 %copy-start.9 = (bf16[4,24,8,512]{3,2,0,1:T(8,128)(2,1)S(1)}, bf16[4,24,8,512]{3,2,0,1:T(8,128)(2,1)}, u32[]{:S(2)}) copy-start(bf16[4,24,8,512]{3,2,0,1:T(8,128)(2,1)} %copy.59) | copy-start | bytes 2359300
Sparse Core Ops, SparseCore 0:
  24.6 190.0 all-reduce.4
  240.1 110.7 reduce-scatter.1
Sparse Core Ops, SparseCore 1:
  154.7 64.6 all-gather.3
  242.0 127.3 all-gather.7
  371.4 95.8 all-gather.5
where the time goes:
time: 499 us; the launch traced here: 490 us
  waiting for transfers between devices  164 us (33%)
  matrix products  131 us (26%)
  blocking collectives  84.5 us (17%)
  local copies, waits for them, and re-layouts  58.4 us (12%)
  other arithmetic  22.3 us (4%)
  between operations  16.1 us (3%)
  starting transfers between devices  14.5 us (3%)
    psum x1, blocking collectives, body(): sum_attn, sum_hidden = lax.psum((part_attn, part_hidden), 'row')  79.4 us
    all_to_all x1, waiting for transfers between devices, body(): lax.all_to_all(normed_b, 'dp', split_axis=1, concat_axis=0, tiled=True)  67 us
    all_gather x1, waiting for transfers between devices, body(): pre_piece = lax.all_gather(grad_pre, 'dp', axis=0, tiled=True)  41.8 us
    unnamed x27, local copies, waits for them, and re-layouts  31 us
    psum x1, waiting for transfers between devices, body(): sum_attn, sum_hidden = lax.psum((part_attn, part_hidden), 'row')  27.9 us
    dot_general x1, matrix products, body(): jnp.einsum('tf,df->td', grad_pre, weight_up, preferred_element_type=f32)  17.5 us
    dot_general x1, matrix products, body(): jnp.einsum('td,fd->tf', cotangent, weight_down, preferred_element_type=f32)  16.4 us
    dot_general x1, matrix products, body(): jnp.einsum('tf,td->fd', moved_hidden, cot_piece, preferred_element_type=f32)  15.5 us
  transfers between devices with their start and end apart: 8, of which 5 were waited for; matrix products, arithmetic and copies ran while one was open for 36% of the time, Pallas kernels for 0%

commit v1 on v0

--- a/solution.py
+++ b/solution.py
@@ -115,9 +115,27 @@
     )
     cot_piece = lax.all_gather(cotangent, "dp", axis=0, tiled=True)
     flat_piece = lax.all_gather(grad_flat, "dp", axis=0, tiled=True)
-    pre_piece = lax.all_gather(grad_pre, "dp", axis=0, tiled=True)
     new_qkv = jnp.einsum("td,ta->da", moved_normed, flat_piece, preferred_element_type=f32)
-    new_up = jnp.einsum("td,tf->df", moved_normed, pre_piece, preferred_element_type=f32)
+    val2 = lax.axis_size("dp")
+    field_out, w1, x_new = (val2, lax.axis_index("dp"), grad_pre.shape[0])
+    so_far_all = tuple(((dev, (dev + 1) % field_out) for dev in range(field_out)))
+    value_now, new_up = (grad_pre, None)
+    no = 0
+    while no < field_out:
+        f_next = (
+            lax.ppermute(value_now, axis_name="dp", perm=so_far_all) if no < field_out - 1 else None
+        )
+        block_out = jnp.einsum(
+            "td,tf->df",
+            lax.dynamic_slice_in_dim(
+                moved_normed, (w1 - no) % field_out * x_new, value_now.shape[0], axis=0
+            ),
+            value_now,
+            preferred_element_type=f32,
+        )
+        new_up = block_out if new_up is None else new_up + block_out
+        value_now = f_next
+        no = no + 1
     new_attn = jnp.einsum("ta,td->ad", moved_attended, cot_piece, preferred_element_type=f32)
     new_down = jnp.einsum("tf,td->fd", moved_hidden, cot_piece, preferred_element_type=f32)
     grad_qkv = new_qkv.astype(bf16).reshape(1, 1, new_qkv.shape[0], 3, head_cols)

time: 499 us -> 539 us (1.080)
  matrix products: 131 us -> 156 us
  starting transfers between devices: 14.5 us -> 27.1 us
    ppermute x0 -> x3, waiting for transfers between devices: none -> 128 us  [body(): lax.ppermute(value_now, axis_name='dp', perm=so_far_all)]
    all_to_all x1, waiting for transfers between devices: 67 us -> 8.42 us  [body(): lax.all_to_all(normed_b, 'dp', split_axis=1, concat_axis=0, tiled=True)]
    all_gather x1 -> x0, waiting for transfers between devices: 41.8 us -> none  [body(): pre_piece = lax.all_gather(grad_pre, 'dp', axis=0, tiled=True)]
    dot_general x1 -> x4, matrix products: 15.3 us -> 41 us  [body(): jnp.einsum('td,tf->df', lax.dynamic_slice_in_dim(moved_normed, (w1 - no)...]
    all_to_all x1, waiting for transfers between devices: 14.6 us -> 0.01 us  [body(): lax.all_to_all(attended, 'dp', split_axis=1, concat_axis=0, tiled=True)]
    all_to_all x1, waiting for transfers between devices: 11.4 us -> 0.01 us  [body(): lax.all_to_all(hidden_b, 'dp', split_axis=1, concat_axis=0, tiled=True)]
    all_to_all x1, starting transfers between devices: 4.66 us -> 10.8 us  [body(): lax.all_to_all(hidden_b, 'dp', split_axis=1, concat_axis=0, tiled=True)]
    all_to_all x1, starting transfers between devices: 4.93 us -> 10.4 us  [body(): lax.all_to_all(normed_b, 'dp', split_axis=1, concat_axis=0, tiled=True)]
  transfers between devices with their start and end apart: 8 -> 10, of which waited for: 5 -> 5; matrix products, arithmetic and copies ran while one was open for 36% -> 37% of each run, Pallas kernels for 0% -> 0%
where the time goes in v1:
time: 539 us; the launch traced here: 530 us
  waiting for transfers between devices  165 us (31%)
  matrix products  156 us (29%)
  blocking collectives  84.4 us (16%)
  local copies, waits for them, and re-layouts  59.1 us (11%)
  starting transfers between devices  27.1 us (5%)
  other arithmetic  22.6 us (4%)
  between operations  16 us (3%)
    ppermute x3, waiting for transfers between devices, body(): lax.ppermute(value_now, axis_name='dp', perm=so_far_all)  128 us
    psum x1, blocking collectives, body(): sum_attn, sum_hidden = lax.psum((part_attn, part_hidden), 'row')  79.4 us
    dot_general x4, matrix products, body(): jnp.einsum('td,tf->df', lax.dynamic_slice_in_dim(moved_normed, (w1 - no)...  41 us
    unnamed x25, local copies, waits for them, and re-layouts  31.8 us
    psum x1, waiting for transfers between devices, body(): sum_attn, sum_hidden = lax.psum((part_attn, part_hidden), 'row')  27.9 us
    dot_general x1, matrix products, body(): jnp.einsum('tf,df->td', grad_pre, weight_up, preferred_element_type=f32)  17.3 us
    dot_general x1, matrix products, body(): jnp.einsum('td,fd->tf', cotangent, weight_down, preferred_element_type=f32)  16.4 us
    dot_general x1, matrix products, body(): jnp.einsum('tf,td->fd', moved_hidden, cot_piece, preferred_element_type=f32)  15.4 us
  transfers between devices with their start and end apart: 10, of which 5 were waited for; matrix products, arithmetic and copies ran while one was open for 37% of the time, Pallas kernels for 0%

profile of v1, /device:TPU:0, one launch (start us, length us, event | category | flops | bytes accessed | tf_op | source)
XLA Modules:
  0.0 529.7 jit_solution(7635151967474739453)
XLA Ops:
  8.0 16.4 %fusion.98 = f32[512,3072]{1,0:T(8,128)} fusion(bf16[512,3072]{1,0:T(8,128)(2,1)} %param.11, bf16[3072,3072]{1,0:T(8,128)(2,1)} %param.15), kind=kOutput, calls=%fused_computation.121 | convolution fusion | flops 9663676416 | bytes 28311552 | tf_op jit(solution)/shard_map/td,fd->tf/dot_general | solution.py:73
  24.5 7.2 %fusion.96 = f32[512,768]{1,0:T(8,128)} fusion(bf16[512,3072]{1,0:T(8,128)(2,1)} %param.11, bf16[768,3072]{1,0:T(8,128)(2,1)} %param.14), kind=kOutput, calls=%fused_computation.119 | convolution fusion | flops 2415919104 | bytes 9437184 | tf_op jit(solution)/shard_map/td,ad->ta/dot_general | solution.py:72
  32.7 79.4 %all-reduce.6 = (bf16[512,768]{1,0:T(8,128)(2,1)S(1)}, f32[512]{0:T(512)S(1)}, f32[512]{0:T(512)S(1)}) all-reduce(f32[512,768]{1,0:T(8,128)} %fusion.96, f32[512]{0:T(512)S(1)} %get-tuple-element.16, f32[512]{0:T(512)S(1)} %get-tuple-element.15), channel_id=1, replica_groups=mesh['dp'=4,'row'=2,'col'=4] {'row'}, use_global_device_ids=true, to_apply=%region_9.0 | all-reduce | flops 394240 | bytes 2367488 | tf_op jit(solution)/shard_map/psum | solution.py:74
  118.7 3.8 fusion.91
  130.4 7.8 %bitcast_reduce_fusion = (f32[2,256,6]{1,2,0:T(8,128)S(1)}, f32[2,256,6]{1,2,0:T(8,128)S(1)}, f32[2,6,128,256]{3,2,1,0:T(8,128)}) fusion(f32[2,256,6]{1,2,0:T(8,128)S(1)} %add_rsqrt_fusion, f32[2,256,6]{1,2,0:T(8,128)S(1)} %broadcast_multiply_fusion.4, bf16[2,256,1,6,128]{1,0,4,3,2:T(2,128)(2,1)S(1)} %get-tuple-element.34, f32[2,6,256,256]{2,3,1,0:T(8,128)} %fusion.55, ...), kind=kOutput, calls=%fused_computation.66 | convolution fusion | flops 212333824 | bytes 9523200 | tf_op jit(solution)/shard_map/bhqk,bqhd->bkhd/dot_general | solution.py:85
  138.2 7.7 %bitcast_reduce_fusion.1 = (f32[2,256,6]{1,2,0:T(8,128)S(1)}, f32[2,256,6]{1,2,0:T(8,128)S(1)}, f32[2,6,128,256]{3,2,1,0:T(8,128)}) fusion(f32[2,256,6]{1,2,0:T(8,128)S(1)} %add_rsqrt_fusion.1, f32[2,256,6]{1,2,0:T(8,128)S(1)} %broadcast_multiply_fusion.5, bf16[2,256,1,6,128]{1,0,4,3,2:T(2,128)(2,1)S(1)} %get-tuple-element.33, ...), kind=kOutput, calls=%fused_computation.68 | convolution fusion | flops 212333824 | bytes 9523200 | tf_op jit(solution)/shard_map/bhqk,bkhd->bqhd/dot_general | solution.py:84
  154.6 19.5 %copy.38 = bf16[3072,3,768]{0,2,1:T(8,128)(2,1)} copy(bf16[3072,3,768]{2,0,1:T(8,128)(2,1)} %param.12) | data formatting | bytes 28311552 | tf_op args[4]
  174.1 12.7 %fusion.97 = f32[512,3072]{1,0:T(8,128)} fusion(bf16[512,2304]{0,1:T(8,128)(2,1)S(1)} %bitcast.154, bf16[3072,2304]{0,1:T(8,128)(2,1)} %bitcast.149), kind=kOutput, calls=%fused_computation.120 | convolution fusion | flops 7247757312 | bytes 22806528 | tf_op jit(solution)/shard_map/ta,da->td/dot_general | solution.py:93
  186.8 27.9 %all-reduce.5.cloned.1.call-done = f32[512,3072]{1,0:T(8,128)} async-done(((f32[512,3072]{1,0:T(8,128)}), f32[512,3072]{1,0:T(8,128)}) %all-reduce.5.cloned.1.call-update) | async-done | bytes 6291472 | tf_op jit(solution)/shard_map/psum | solution.py:74
  214.6 8.9 %fusion.11 = (bf16[512,3072]{1,0:T(8,128)(2,1)}, bf16[512,3072]{1,0:T(8,128)(2,1)}) fusion(bf16[512,3072]{1,0:T(8,128)(2,1)} %param.10, f32[512,3072]{1,0:T(8,128)} %all-reduce.5.cloned.1.call-done), kind=kLoop, calls=%fused_computation.20 | loop fusion | flops 22020096 | bytes 15728640 | tf_op jit(solution)/shard_map/convert_element_type | solution.py:71
  223.5 17.3 %convolution_add_fusion = f32[512,3072]{1,0:T(8,128)} fusion(f32[512,3072]{1,0:T(8,128)} %fusion.97, bf16[512,3072]{1,0:T(8,128)(2,1)} %get-tuple-element.31, bf16[3072,3072]{1,0:T(8,128)(2,1)} %param.13), kind=kOutput, calls=%fused_computation.23 | convolution fusion | flops 9665249280 | bytes 34603008 | tf_op jit(solution)/shard_map/tf,df->td/dot_general | solution.py:95
  242.0 3.6 fusion.51
  245.6 3.9 copy.42
  249.5 3.2 all_to_all.46
  252.7 4.3 all-to-all-start.1
  257.0 71.3 %collective-permute-done = bf16[512,3072]{1,0:T(8,128)(2,1)} collective-permute-done((bf16[512,3072]{1,0:T(8,128)(2,1)}, bf16[512,3072]{1,0:T(8,128)(2,1)}, u32[]{:S(2)}, u32[]{:S(2)}) %collective-permute-start) | collective-permute-done | bytes 3145760 | tf_op jit(solution)/shard_map/ppermute | solution.py:126
  329.8 4.0 fusion.83
  335.6 10.4 %all-to-all-start = ((bf16[512,4,768]{2,0,1:T(8,128)(2,1)}), bf16[512,4,768]{2,0,1:T(8,128)(2,1)}, u32[]{:S(2)}, u32[]{:S(2)}) async-start(bf16[512,4,768]{2,0,1:T(8,128)(2,1)} %bitcast.148), calls=%async_computation.1 | async-start | bytes 6291456 | tf_op jit(solution)/shard_map/all_to_all | solution.py:112
  350.1 54.8 %collective-permute-done.1 = bf16[512,3072]{1,0:T(8,128)(2,1)} collective-permute-done((bf16[512,3072]{1,0:T(8,128)(2,1)}, bf16[512,3072]{1,0:T(8,128)(2,1)}, u32[]{:S(2)}, u32[]{:S(2)}) %collective-permute-start.1) | collective-permute-done | bytes 3145760 | tf_op jit(solution)/shard_map/ppermute | solution.py:126
  404.9 8.4 %all-to-all-done = bf16[512,4,768]{2,0,1:T(8,128)(2,1)} async-done(((bf16[512,4,768]{2,0,1:T(8,128)(2,1)}), bf16[512,4,768]{2,0,1:T(8,128)(2,1)}, u32[]{:S(2)}, u32[]{:S(2)}) %all-to-all-start) | async-done | bytes 3145760 | tf_op jit(solution)/shard_map/all_to_all | solution.py:112
  413.3 10.8 %all-to-all-start.2 = ((bf16[512,4,768]{2,0,1:T(8,128)(2,1)}), bf16[512,4,768]{2,0,1:T(8,128)(2,1)}, u32[]{:S(2)}, u32[]{:S(2)}) async-start(bf16[512,4,768]{2,0,1:T(8,128)(2,1)} %bitcast.147), calls=%async_computation.3 | async-start | bytes 6291456 | tf_op jit(solution)/shard_map/all_to_all | solution.py:114
  424.1 8.4 %fusion.62 = f32[768,3072]{1,0:T(8,128)} fusion(bf16[512,3072]{1,0:T(8,128)(2,1)} %get-tuple-element.31, bf16[2048,768]{1,0:T(8,128)(2,1)} %bitcast.11, s32[]{:T(128)S(6)} %select_n.38), kind=kOutput, calls=%fused_computation.87 | convolution fusion | flops 2415919104 | bytes 13369348 | tf_op jit(solution)/shard_map/td,tf->df/dot_general | solution.py:128
  432.5 8.3 %fusion.60 = f32[768,3072]{1,0:T(8,128)} fusion(bf16[512,3072]{1,0:T(8,128)(2,1)} %collective-permute-done, bf16[2048,768]{1,0:T(8,128)(2,1)} %bitcast.11, s32[]{:T(128)S(6)} %select_n.40), kind=kOutput, calls=%fused_computation.85 | convolution fusion | flops 2415919104 | bytes 13369348 | tf_op jit(solution)/shard_map/td,tf->df/dot_general | solution.py:128
  440.8 8.4 %fusion.58 = f32[768,3072]{1,0:T(8,128)} fusion(bf16[512,3072]{1,0:T(8,128)(2,1)} %collective-permute-done.1, bf16[2048,768]{1,0:T(8,128)(2,1)} %bitcast.11, s32[]{:T(128)S(6)} %select_n.42), kind=kOutput, calls=%fused_computation.83 | convolution fusion | flops 2415919104 | bytes 13369348 | tf_op jit(solution)/shard_map/td,tf->df/dot_general | solution.py:128
  449.3 13.2 %convolution_convert_fusion.1 = bf16[768,2304]{1,0:T(8,128)(2,1)} fusion(bf16[2048,768]{1,0:T(8,128)(2,1)} %bitcast.11, bf16[2048,2304]{0,1:T(8,128)(2,1)} %all-gather.3.cloned.1.call-done), kind=kOutput, calls=%fused_computation.22 | convolution fusion | flops 7249526784 | bytes 16121856 | tf_op jit(solution)/shard_map/td,ta->da/dot_general | solution.py:118
  462.4 4.5 copy.40
  466.9 3.9 copy.45
  472.3 15.9 %fusion.13 = bf16[1,1,768,3072]{3,2,1,0:T(8,128)(2,1)} fusion(bf16[512,3072]{1,0:T(8,128)(2,1)} %collective-permute-done.2, f32[768,3072]{1,0:T(8,128)} %fusion.58, f32[768,3072]{1,0:T(8,128)} %fusion.62, f32[768,3072]{1,0:T(8,128)} %fusion.60, bf16[2048,768]{1,0:T(8,128)(2,1)} %bitcast.11, s32[]{:T(128)S(6)} %select_n.44), kind=kOutput, calls=%fused_computation.25 | convolution fusion | flops 2425356288 | bytes 36962308 | tf_op jit(solution)/shard_map/td,tf->df/dot_general | solution.py:128
  490.4 4.9 all-reduce
  495.4 8.2 %fusion.14 = bf16[1,1,192,3072]{3,2,1,0:T(8,128)(2,1)} fusion(bf16[2048,192]{0,1:T(8,128)(2,1)S(1)} %bitcast.156, bf16[2048,3072]{1,0:T(8,128)(2,1)} %all-gather.5.cloned.1.call-done), kind=kOutput, calls=%fused_computation.27 | convolution fusion | flops 2416508928 | bytes 14548992 | tf_op jit(solution)/shard_map/ta,td->ad/dot_general | solution.py:139
  503.6 15.4 %fusion.12 = bf16[1,1,768,3072]{3,2,1,0:T(8,128)(2,1)} fusion(bf16[2048,768]{1,0:T(8,128)(2,1)} %bitcast.19, bf16[2048,3072]{1,0:T(8,128)(2,1)} %all-gather.5.cloned.1.call-done), kind=kOutput, calls=%fused_computation.24 | convolution fusion | flops 9666035712 | bytes 20447232 | tf_op jit(solution)/shard_map/tf,td->fd/dot_general | solution.py:140
  519.0 3.0 add_convert_fusion.1
  (70 shorter events, 36.3 us)
Async XLA Ops:
  8.0 206.6 %all-reduce.5.cloned.1.call-start = ((), (), s32[]{:S(2)}) async-start(), calls=%async_computation.4 | async-start | bytes 12582912 | tf_op jit(solution)/shard_map/psum | solution.py:74
  24.4 7.3 %copy-start = (bf16[512,3072]{1,0:T(8,128)(2,1)S(1)}, bf16[512,3072]{1,0:T(8,128)(2,1)}, u32[]{:S(2)}) copy-start(bf16[512,3072]{1,0:T(8,128)(2,1)} %param.8) | copy-start | bytes 9437188
  24.5 424.8 %all-gather.3.cloned.1.call-start = ((), (), s32[]{:S(2)}) async-start(), calls=%async_computation.6 | async-start | bytes 11796480 | tf_op jit(solution)/shard_map/all_gather | solution.py:117
  124.9 2.9 copy-start.5
  145.8 2.3 copy-start.7
  145.8 3.3 copy-start.9
  154.5 19.6 %copy-start.3 = (bf16[288,8,2,256]{3,1,2,0:T(8,128)(2,1)S(1)}, bf16[288,8,2,256]{3,1,2,0:T(8,128)(2,1)}, u32[]{:S(2)}) copy-start(bf16[288,8,2,256]{3,1,2,0:T(8,128)(2,1)} %copy.60) | copy-start | bytes 7077892
  154.5 333.7 %reduce-scatter.2.cloned.1.call-start = ((), (), s32[]{:S(2)}) async-start(), calls=%async_computation.5 | async-start | bytes 7864320 | tf_op jit(solution)/shard_map/reduce_scatter | solution.py:94
  240.8 1.1 copy-start.6
  240.9 254.5 %all-gather.5.cloned.1.call-start = ((), (), s32[]{:S(2)}) async-start(), calls=%async_computation.7 | async-start | bytes 15728640 | tf_op jit(solution)/shard_map/all_gather | solution.py:116
  241.5 86.9 %collective-permute-start = (bf16[512,3072]{1,0:T(8,128)(2,1)}, bf16[512,3072]{1,0:T(8,128)(2,1)}, u32[]{:S(2)}, u32[]{:S(2)}) collective-permute-start(bf16[512,3072]{1,0:T(8,128)(2,1)} %get-tuple-element.31), channel_id=1, source_target_pairs={{0,8},{8,16},{16,24},{24,0},{1,9},{9,17},{17,25},{25,1},{2,10},{10... | collective-permute-start | bytes 9437192 | tf_op jit(solution)/shard_map/ppermute | solution.py:126
  245.6 84.2 %copy-start.1 = (bf16[512,3072]{1,0:T(8,128)(2,1)S(1)}, bf16[512,3072]{1,0:T(8,128)(2,1)}, u32[]{:S(2)}) copy-start(bf16[512,3072]{1,0:T(8,128)(2,1)} %param.8) | copy-start | bytes 9437188
  252.7 82.9 %all-to-all-start.1 = ((bf16[512,4,192]{0,2,1:T(8,128)(2,1)}), bf16[512,4,192]{0,2,1:T(8,128)(2,1)}, u32[]{:S(2)}, u32[]{:S(2)}) async-start(bf16[512,4,192]{0,2,1:T(8,128)(2,1)} %all_to_all.46), calls=%async_computation.2 | async-start | bytes 1572864 | tf_op jit(solution)/shard_map/all_to_all | solution.py:113
  328.3 76.6 %collective-permute-start.1 = (bf16[512,3072]{1,0:T(8,128)(2,1)}, bf16[512,3072]{1,0:T(8,128)(2,1)}, u32[]{:S(2)}, u32[]{:S(2)}) collective-permute-start(bf16[512,3072]{1,0:T(8,128)(2,1)} %collective-permute-done), channel_id=1, source_target_pairs={{0,8},{8,16},{16,24},{24,0},{1,9},{9,17},{17,25},{25,1},{2,10},{10... | collective-permute-start | bytes 9437192 | tf_op jit(solution)/shard_map/ppermute | solution.py:126
  335.6 12.6 %copy-start.2 = (bf16[512,3072]{1,0:T(8,128)(2,1)S(1)}, bf16[512,3072]{1,0:T(8,128)(2,1)}, u32[]{:S(2)}) copy-start(bf16[512,3072]{1,0:T(8,128)(2,1)} %get-tuple-element.30) | copy-start | bytes 9437188
  335.6 77.7 %all-to-all-start = ((bf16[512,4,768]{2,0,1:T(8,128)(2,1)}), bf16[512,4,768]{2,0,1:T(8,128)(2,1)}, u32[]{:S(2)}, u32[]{:S(2)}) async-start(bf16[512,4,768]{2,0,1:T(8,128)(2,1)} %bitcast.148), calls=%async_computation.1 | async-start | bytes 6291456 | tf_op jit(solution)/shard_map/all_to_all | solution.py:112
  404.9 67.4 %collective-permute-start.2 = (bf16[512,3072]{1,0:T(8,128)(2,1)}, bf16[512,3072]{1,0:T(8,128)(2,1)}, u32[]{:S(2)}, u32[]{:S(2)}) collective-permute-start(bf16[512,3072]{1,0:T(8,128)(2,1)} %collective-permute-done.1), channel_id=1, source_target_pairs={{0,8},{8,16},{16,24},{24,0},{1,9},{9,17},{17,25},{25,1},{2,10},{10... | collective-permute-start | bytes 9437192 | tf_op jit(solution)/shard_map/ppermute | solution.py:126
  413.3 90.2 %all-to-all-start.2 = ((bf16[512,4,768]{2,0,1:T(8,128)(2,1)}), bf16[512,4,768]{2,0,1:T(8,128)(2,1)}, u32[]{:S(2)}, u32[]{:S(2)}) async-start(bf16[512,4,768]{2,0,1:T(8,128)(2,1)} %bitcast.147), calls=%async_computation.3 | async-start | bytes 6291456 | tf_op jit(solution)/shard_map/all_to_all | solution.py:114
  488.2 7.2 %copy-start.8 = (bf16[4,24,8,512]{3,2,0,1:T(8,128)(2,1)S(1)}, bf16[4,24,8,512]{3,2,0,1:T(8,128)(2,1)}, u32[]{:S(2)}) copy-start(bf16[4,24,8,512]{3,2,0,1:T(8,128)(2,1)} %copy.59) | copy-start | bytes 2359300
  503.6 15.4 %copy-start.4 = (f32[128,3072]{1,0:T(8,128)S(1)}, f32[128,3072]{1,0:T(8,128)}, u32[]{:S(2)}) copy-start(f32[128,3072]{1,0:T(8,128)} %reduce-scatter.2.cloned.1.call-done) | copy-start | bytes 4718596
Sparse Core Ops, SparseCore 0:
  24.6 190.0 all-reduce.4
  241.0 110.7 reduce-scatter.1
Sparse Core Ops, SparseCore 1:
  154.6 64.6 all-gather.2
  242.9 123.8 all-gather.4
